TPU v7x, 32 devices: a whole 2x2x4 slice. The times are simulated.
32 devices in a mesh: rows: 4 (over z), cols: 8 (over y, x, core).
Axes of the slice: x: 2, y: 2, z: 4, core: 2. Of those that a mesh axis runs over, the one named last changes fastest.
Arguments:
- pivot_rhs: float32 [4, 4096, 1024], P(None, 'cols'), may hold values from -6 to 6
- bound_sol: bfloat16 [16384, 1024], P('rows'), may hold values from -6 to 6
- border_tiles: bfloat16 [16384, 4, 4096], P('rows', None, 'cols'), may hold values from -0.046875 to 0.046875
- lower_tiles: bfloat16 [6, 4096, 4096], P(None, 'rows', 'cols'), may hold values from -0.09375 to 0.09375
- inverse_diag: bfloat16 [4, 4096, 4096], P(None, 'cols', 'rows'), may hold values from -0.09375 to 0.09375
- owner_map: int32 [32, 512, 1], P(('rows', 'cols')), may hold values from 0 to 31; in each aligned block of 512 rows (0 to 511, 512 to 1023, ..., all dimensions but the last counted through in order) at most 32 rows name the same one
Outputs:
- child_rows: float32 [32768, 1024], P(('rows', 'cols'))
Inputs may be any that keep to these rules, and one draw needn't show every extreme that they name: `owner_map`: among the rows of one device (one index of the first dimension), no owner is named more than 32 times, a bound that some block reaches; every owner is named somewhere.
All inputs are finite; a program needn't handle non-finite values.
Results may differ from a plain program's by a relative error of at most 0.008.
Values may be sent and summed in bfloat16 or wider, within the bound.
A program may use at most 128 MiB of HBM per device.

v0:
```python
import functools

import jax
import jax.numpy as jnp
from jax import lax
from jax.experimental import pallas as pl
from jax.experimental.pallas import tpu as pltpu
from jax.sharding import PartitionSpec as P

MESH = pl.DeviceIdType.MESH
MID_LAGS = (0, 3, 6, 9, 11, 14)
END_LAGS = (0, 0, 8, 10, 12, 14)
LAG_BASE = 15


def solve_kernel(dims, pend_in, lower_in, inv_in, out, pend, lower, inv, xt, part, qbuf, sbuf, recv_a, xbuf, resid,
                 pair_s, pair_r, rs_s, rs_r, s_sem, a_sem, x_sem, b_sem, bs_sem, ps_sem, pr_sem,
                 rss_sem, rsr_sem, ags_sem, agr_sem, fs_sem, fr_sem, o_sem, pl_sem, il_sem, ll_sem):
    R, C, NB, N, PC = dims
    M = C // 2
    HALF = N // 2
    depth = inv.shape[2]
    by_lanes = N // C < 16
    CH = HALF if by_lanes else HALF // M
    LW = depth // M if by_lanes else depth
    S = 2 * PC
    items = NB * PC
    z = lax.axis_index("rows")
    c = lax.axis_index("cols")
    h = lax.rem(c, 2)
    m = c // 2
    low = z < R // 2
    mid = jnp.logical_or(z == R // 2 - 1, z == R // 2)
    edge = jnp.logical_or(z == 0, z == R - 1)
    inner = jnp.where(low, z + 1, z - 1)
    outer = jnp.where(low, z - 1, z + 1)
    outer_safe = jnp.where(edge, inner, outer)
    partner = c + 1 - 2 * h

    def peer(d):
        return 2 * lax.rem(m + d, M) + h

    def share(base, q):
        if by_lanes:
            return pl.ds(pl.multiple_of(base, HALF), HALF), pl.ds(pl.multiple_of(q * LW, LW), LW)
        return pl.ds(pl.multiple_of(base + q * CH, CH), CH), slice(None)

    def load_pend(k):
        return pltpu.make_async_copy(pend_in.at[k], pend.at[k], pl_sem.at[k])

    def load_inv(k):
        return pltpu.make_async_copy(inv_in.at[k], inv.at[k], il_sem.at[k])

    load_lower = pltpu.make_async_copy(lower_in, lower, ll_sem)
    load_pend(NB - 1).start()
    load_inv(NB - 1).start()
    load_lower.start()
    for k in range(NB - 2, -1, -1):
        load_pend(k).start()
        load_inv(k).start()

    barrier = pltpu.get_barrier_semaphore()

    @pl.when(z > 0)
    def _():
        pl.semaphore_signal(barrier, inc=1, device_id={"rows": z - 1}, device_id_type=MESH)

    @pl.when(z < R - 1)
    def _():
        pl.semaphore_signal(barrier, inc=1, device_id={"rows": z + 1}, device_id_type=MESH)

    pl.semaphore_signal(barrier, inc=1, device_id={"cols": partner}, device_id_type=MESH)
    for d in range(1, M):
        pl.semaphore_signal(barrier, inc=1, device_id={"cols": peer(d)}, device_id_type=MESH)
    pl.semaphore_wait(barrier, M + jnp.where(edge, 1, 2))

    def remote(src, dst, ss, rs, where):
        return pltpu.make_async_remote_copy(src_ref=src, dst_ref=dst, send_sem=ss, recv_sem=rs,
                                            device_id=where, device_id_type=MESH)

    def inner_copy(s):
        return remote(sbuf.at[s], recv_a.at[s], s_sem.at[s], a_sem.at[s], {"rows": inner})

    def swap_copy(s):
        return remote(sbuf.at[s], xbuf.at[s], s_sem.at[s], x_sem.at[s], {"rows": inner})

    def back_copy(s):
        return remote(resid.at[s], resid.at[s], bs_sem.at[s], b_sem.at[s], {"rows": outer_safe})

    def pair_copy(s):
        return remote(pair_s.at[s], pair_r.at[s], ps_sem.at[s], pr_sem.at[s], {"cols": partner})

    def rs_copy(s, d):
        rows, lanes = share(0, lax.rem(m + d, M))
        return remote(rs_s.at[s, rows, lanes], rs_r.at[s, d - 1], rss_sem.at[s, d - 1], rsr_sem.at[s, d - 1],
                      {"cols": peer(d)})

    def ag_copy(s, k, p, d):
        rows, lanes = share(p * N + h * HALF, m)
        return remote(xt.at[k, rows, lanes], xt.at[k, rows, lanes], ags_sem.at[s, d - 1], agr_sem.at[s, d - 1],
                      {"cols": peer(d)})

    def fwd_copy(s, k, p):
        rows = pl.ds(pl.multiple_of(p * N + h * HALF, HALF), HALF)
        return remote(xt.at[k, rows], xt.at[k, rows], fs_sem.at[s], fr_sem.at[s], {"cols": partner})

    def split(i):
        k = NB - 1 - i // PC
        return k, lax.rem(i, PC), lax.rem(i, S)

    def piece(p):
        return pl.ds(pl.multiple_of(p * N, N), N)

    def first(i):
        k, p, s = split(i)

        @pl.when(i >= PC)
        def _():
            kb, pb, sb = split(i - PC)
            fwd_copy(sb, kb, pb).wait_recv()

        @pl.when(p == 0)
        def _():
            load_pend(k).wait()

        @pl.when(i == PC)
        def _():
            load_lower.wait()

        part[p] = pend[k, piece(p), :]

        def add(j, carry):
            part[p] += jnp.dot(xt[j, piece(p), :], lower[j * (j - 1) // 2 + k],
                               preferred_element_type=jnp.float32)
            return carry

        lax.fori_loop(k + 1, NB, add, 0)

        @pl.when(edge)
        def _():
            sbuf[s] = part[p].astype(jnp.bfloat16)
            inner_copy(s).start()

    def second(i):
        k, p, s = split(i)

        @pl.when(jnp.logical_not(edge))
        def _():
            inner_copy(s).wait_recv()
            part[p] += recv_a[s].astype(jnp.float32)
            sbuf[s] = part[p].astype(jnp.bfloat16)

            @pl.when(mid)
            def _():
                swap_copy(s).start()

            @pl.when(jnp.logical_not(mid))
            def _():
                inner_copy(s).start()

    def third(i):
        k, p, s = split(i)

        @pl.when(mid)
        def _():
            swap_copy(s).wait_recv()
            resid[s] = (-(part[p] + xbuf[s].astype(jnp.float32))).astype(jnp.bfloat16)

        @pl.when(jnp.logical_not(mid))
        def _():
            back_copy(s).wait_recv()

        @pl.when(jnp.logical_not(edge))
        def _():
            back_copy(s).start()

        @pl.when(p == 0)
        def _():
            load_inv(k).wait()

        qbuf[p] = jnp.dot(resid[s], inv[k], preferred_element_type=jnp.float32)
        theirs = pl.ds(pl.multiple_of((1 - h) * HALF, HALF), HALF)
        pair_s[s] = qbuf[p, theirs, :].astype(jnp.bfloat16)
        pair_copy(s).start()

    def fourth(i):
        k, p, s = split(i)
        pair_copy(s).wait_recv()
        mine = pl.ds(pl.multiple_of(h * HALF, HALF), HALF)
        both = qbuf[p, mine, :] + pair_r[s].astype(jnp.float32)
        qbuf[p, mine, :] = both
        rs_s[s] = both.astype(jnp.bfloat16)
        for d in range(1, M):
            rs_copy(s, d).start()

    def fifth(i):
        k, p, s = split(i)
        rows, lanes = share(h * HALF, m)
        total = qbuf[p, rows, lanes]
        for d in range(1, M):
            rs_copy(s, d).wait_recv()
        for d in range(1, M):
            total = total + rs_r[s, d - 1].astype(jnp.float32)
        rows, lanes = share(p * N + h * HALF, m)
        xt[k, rows, lanes] = total.astype(jnp.bfloat16)
        for d in range(1, M):
            ag_copy(s, k, p, d).start()

    def sixth(i):
        k, p, s = split(i)
        for d in range(1, M):
            ag_copy(s, k, p, d).wait_recv()
        fwd_copy(s, k, p).start()

    def sends(i):
        k, p, s = split(i)
        inner_copy(s).wait_send()

        @pl.when(jnp.logical_not(edge))
        def _():
            back_copy(s).wait_send()

        pair_copy(s).wait_send()
        for d in range(1, M):
            rs_copy(s, d).wait_send()
        for d in range(1, M):
            ag_copy(s, k, p, d).wait_send()
        fwd_copy(s, k, p).wait_send()

    mid_lags = [min(lag, LAG_BASE) * (PC - 1) // LAG_BASE for lag in MID_LAGS]
    end_lags = [min(lag, LAG_BASE) * (PC - 1) // LAG_BASE for lag in END_LAGS]
    stages = list(zip((first, second, third, fourth, fifth, sixth), mid_lags, end_lags))
    stages.append((sends, PC + PC // 2, PC + PC // 2))

    def step(t, carry):
        for stage, mid_lag, end_lag in stages:
            i = t - jnp.where(mid, mid_lag, end_lag)

            @pl.when(jnp.logical_and(i >= 0, i < items))
            def _(stage=stage, i=i):
                stage(i)
        return carry

    lax.fori_loop(0, items + PC + PC // 2, step, 0)

    def last(i, carry):
        k, p, s = split(i)
        fwd_copy(s, k, p).wait_recv()
        return carry

    lax.fori_loop(items - PC, items, last, 0)
    cut = out.shape[2]
    source = xt
    if cut < depth:
        source = xt.at[:, :, pl.ds(pl.multiple_of(c * cut, cut), cut)]
    write = pltpu.make_async_copy(source, out, o_sem)
    write.start()
    write.wait()


def solve(pend, lower, inv, R, C):
    NB, sources, width = pend.shape
    depth = inv.shape[2]
    wide = depth % (64 * C) == 0
    N = min(8 * C if wide else 16 * C, sources // 2)
    PC = sources // N
    S = 2 * PC
    M = C // 2
    bf, f32 = jnp.bfloat16, jnp.float32
    dma = pltpu.SemaphoreType.DMA
    anywhere = pl.BlockSpec(memory_space=pl.ANY)
    cut = depth // C if depth % (128 * C) == 0 else depth
    return pl.pallas_call(
        functools.partial(solve_kernel, (R, C, NB, N, PC)),
        out_shape=jax.ShapeDtypeStruct((NB, sources, cut), bf),
        in_specs=[anywhere, anywhere, anywhere],
        out_specs=pl.BlockSpec(memory_space=pl.ANY),
        scratch_shapes=[
            pltpu.VMEM(pend.shape, f32),
            pltpu.VMEM(lower.shape, bf),
            pltpu.VMEM(inv.shape, bf),
            pltpu.VMEM((NB, sources, depth), bf),
            pltpu.VMEM((PC, N, width), f32),
            pltpu.VMEM((PC, N, depth), f32),
            pltpu.VMEM((S, N, width), bf),
            pltpu.VMEM((S, N, width), bf),
            pltpu.VMEM((S, N, width), bf),
            pltpu.VMEM((S, N, width), bf),
            pltpu.VMEM((S, N // 2, depth), bf),
            pltpu.VMEM((S, N // 2, depth), bf),
            pltpu.VMEM((S, N // 2, depth), bf),
            pltpu.VMEM((S, M - 1) + ((N // 2, depth // M) if N // C < 16 else (N // C, depth)), bf),
            dma((S,)), dma((S,)), dma((S,)), dma((S,)), dma((S,)), dma((S,)), dma((S,)),
            dma((S, M - 1)), dma((S, M - 1)), dma((S, M - 1)), dma((S, M - 1)),
            dma((S,)), dma((S,)), dma, dma((NB,)), dma((NB,)), dma,
        ],
        compiler_params=pltpu.CompilerParams(
            collective_id=0, has_side_effects=True, vmem_limit_bytes=60 * 1024 * 1024
        ),
    )(pend, lower, inv)


def local(pivot_rhs, bound_sol, border_tiles, lower_tiles, inverse_diag, owner_map):
    R = lax.axis_size("rows")
    C = lax.axis_size("cols")
    devices = R * C
    blocks, _, sources = pivot_rhs.shape
    rows_dev = owner_map.shape[1]
    per_block = rows_dev // blocks
    most = max(2, 2 * rows_dev // devices)
    border = lax.dot_general(
        bound_sol, border_tiles, (((0,), (0,)), ((), ())), preferred_element_type=jnp.float32
    )
    row = lax.axis_index("rows")
    if R % blocks == 0:
        block = row // (R // blocks)
        mine = jnp.logical_and(jnp.arange(blocks) == block, lax.rem(row, R // blocks) == 0)
        rhs = lax.dynamic_index_in_dim(pivot_rhs, block, 0, keepdims=False).T[None]
        rhs = jnp.where(mine[:, None, None], rhs, 0.0)
    else:
        rhs = jnp.where(row == R // 2 - 1, pivot_rhs.transpose(0, 2, 1), 0.0)
    pend = border.transpose(1, 0, 2) - rhs
    xt = solve(pend, lower_tiles, inverse_diag, R, C)

    own = xt
    if xt.shape[2] > per_block:
        own = lax.dynamic_slice_in_dim(xt, lax.axis_index("cols") * per_block, per_block, axis=2)
    owners = owner_map[0, :, 0]
    onehot = (owners[:, None] == jnp.arange(devices, dtype=jnp.int32)[None, :]).astype(jnp.int32)
    ranks = jnp.cumsum(onehot, axis=0) - onehot
    slots = jnp.sum(ranks * onehot, axis=1)
    target = owners * most + slots
    select = (jnp.arange(devices * most, dtype=jnp.int32)[:, None] == target[None, :]).astype(jnp.bfloat16)
    select = select.reshape(devices * most, blocks, per_block)
    packed = lax.dot_general(
        select, own, (((1, 2), (0, 2)), ((), ())), preferred_element_type=jnp.float32
    ).astype(jnp.bfloat16)
    received = lax.all_to_all(
        packed.reshape(devices, most, sources), ("rows", "cols"), split_axis=0, concat_axis=0, tiled=True
    )
    return received.reshape(devices * most, sources).astype(jnp.float32)


def solution(mesh):
    placed = (
        P(None, "cols", None),
        P("rows", None),
        P("rows", None, "cols"),
        P(None, "rows", "cols"),
        P(None, "cols", "rows"),
        P(("rows", "cols"), None, None),
    )
    return jax.shard_map(
        local, mesh=mesh, in_specs=placed, out_specs=P(("rows", "cols"), None), check_vma=False
    )
```

profile of v0, /device:TPU:0, one launch (start us, length us, event | category | flops | bytes accessed | tf_op | source)
XLA Modules:
  0.0 220.6 jit_solution(9091660653527048287)
XLA Ops:
  0.0 0.0 copy-start
  0.0 1.7 dynamic-slice_bitcast_fusion
  1.7 1.8 copy.8
  3.6 0.0 copy-done
  3.6 1.2 reduce-window.6
  4.7 0.2 slice_reduce_fusion
  5.0 0.1 fusion.6
  5.1 24.5 %bitcast_subtract_fusion.pend_in = f32[4,1024,512]{2,1,0:T(8,128)} fusion(f32[1024,512]{1,0:T(8,128)} %copy.8, pred[4]{0:T(512)(128)(4,1)S(1)} %iota_compare_fusion.4, bf16[4096,4,512]{2,1,0:T(4,128)(2,1)} %param.8, bf16[4096,1024]{1,0:T(8,128)(2,1)} %param.7), kind=kOutput, calls=%fused_computation.2 | convolution fusion | flops 17184063488 | bytes 35651588 | tf_op jit(solution)/shard_map/dot_general | solution.py:311
  29.6 133.1 %shard_map.64 = bf16[4,1024,128]{2,1,0:T(8,128)(2,1)} custom-call(f32[4,1024,512]{2,1,0:T(8,128)} %bitcast_subtract_fusion.pend_in, bf16[6,1024,512]{2,1,0:T(8,128)(2,1)} %lower_in.1, bf16[4,512,1024]{2,1,0:T(8,128)(2,1)} %inv_in.1), custom_call_target="tpu_custom_call" | custom-call | tf_op jit(solution)/shard_map/pallas_call | solution.py:273
  162.7 2.5 %bitcast_convert_fusion = bf16[1024,1024]{1,0:T(8,128)(2,1)S(1)} fusion(bf16[4,1024,128]{2,1,0:T(8,128)(2,1)} %shard_map.64, s32[4,128]{1,0:T(4,128)S(1)} %bitcast_add_fusion), kind=kOutput, calls=%fused_computation.4 | convolution fusion | flops 1075314688 | bytes 3147776 | tf_op jit(solution)/shard_map/dot_general | solution.py:335
  165.2 52.8 %all_to_all.5 = bf16[32,32,1024]{2,1,0:T(8,128)(2,1)S(1)} all-to-all(bf16[32,32,1024]{2,1,0:T(8,128)(2,1)S(1)} %bitcast.41), channel_id=1, replica_groups=mesh['rows'=4,'cols'=8] {'rows','cols'}, dimensions={0} | all-to-all | bytes 4194304 | tf_op jit(solution)/shard_map/all_to_all | solution.py:338
  218.0 2.6 %bitcast_convert_fusion.1 = f32[1024,1024]{1,0:T(8,128)} fusion(bf16[32,32,1024]{2,1,0:T(8,128)(2,1)S(1)} %all_to_all.5), kind=kLoop, calls=%fused_computation.5 | loop fusion | flops 1048576 | bytes 6291456 | tf_op jit(solution)/shard_map/convert_element_type | solution.py:341
  (5 shorter events, 0.1 us)
Async XLA Ops:
  0.0 3.6 %copy-start = (s32[1,512,1]{1,2,0:T(1,128)S(1)}, s32[1,512,1]{1,2,0:T(1,128)}, u32[]{:S(2)}) copy-start(s32[1,512,1]{1,2,0:T(1,128)} %param.11) | copy-start | bytes 6148
where the time goes:
time: 221 us
  Pallas kernels  133 us (60%)
  blocking collectives  52.8 us (24%)
  matrix products  27 us (12%)
  other arithmetic  3.95 us (2%)
  local copies, waits for them, and re-layouts  3.78 us (2%)
    pallas_call x1, Pallas kernels, solve(): pl.pallas_call(functools.partial(solve_kernel, (R, C, NB, N, PC)), out_sh...  133 us
    all_to_all x1, blocking collectives, local(): lax.all_to_all(packed.reshape(devices, most, sources), ('rows', 'cols'),...  52.8 us
    dot_general x1, matrix products, local(): lax.dot_general(bound_sol, border_tiles, (((0,), (0,)), ((), ())), prefer...  24.5 us

commit v1 on v0

--- a/solution.py
+++ b/solution.py
@@ -11,6 +11,7 @@
 MID_LAGS = (0, 3, 6, 9, 11, 14)
 END_LAGS = (0, 0, 8, 10, 12, 14)
 LAG_BASE = 15
+GROUP = 4
 
 
 def solve_kernel(dims, pend_in, lower_in, inv_in, out, pend, lower, inv, xt, part, qbuf, sbuf, recv_a, xbuf, resid,
@@ -300,6 +301,373 @@
     )(pend, lower, inv)
 
 
+def fused_kernel(dims, pend_in, lower_in, inv_in, target, out, pend, lower, inv, xt, part, qbuf, sbuf, recv_a, xbuf, resid,
+                 pair_s, pair_r, rs_s, rs_r, s_sem, a_sem, x_sem, b_sem, bs_sem, ps_sem, pr_sem,
+                 rss_sem, rsr_sem, ags_sem, agr_sem, fs_sem, fr_sem, o_sem, pl_sem, il_sem, ll_sem,
+                 select, own, pack, recv, ks_sem, kr_sem):
+    R, C, NB, N, PC, most = dims
+    devices = R * C
+    M = C // 2
+    HALF = N // 2
+    depth = inv.shape[2]
+    LW = depth // M
+    LB = depth // C
+    G, slots, GW = pack.shape
+    PG = GW // N
+    S = 2 * PC
+    items = NB * PC
+    z = lax.axis_index("rows")
+    c = lax.axis_index("cols")
+    h = lax.rem(c, 2)
+    m = c // 2
+    low = z < R // 2
+    mid = jnp.logical_or(z == R // 2 - 1, z == R // 2)
+    edge = jnp.logical_or(z == 0, z == R - 1)
+    inner = jnp.where(low, z + 1, z - 1)
+    outer = jnp.where(low, z - 1, z + 1)
+    outer_safe = jnp.where(edge, inner, outer)
+    partner = c + 1 - 2 * h
+    me = z * C + c
+
+    def peer(d):
+        return 2 * lax.rem(m + d, M) + h
+
+    def share(base, q):
+        return pl.ds(pl.multiple_of(base, HALF), HALF), pl.ds(pl.multiple_of(q * LW, LW), LW)
+
+    def load_pend(k):
+        return pltpu.make_async_copy(pend_in.at[k], pend.at[k], pl_sem.at[k])
+
+    def load_inv(k):
+        return pltpu.make_async_copy(inv_in.at[k], inv.at[k], il_sem.at[k])
+
+    load_lower = pltpu.make_async_copy(lower_in, lower, ll_sem)
+    load_pend(NB - 1).start()
+    load_inv(NB - 1).start()
+    load_lower.start()
+    for k in range(NB - 2, -1, -1):
+        load_pend(k).start()
+        load_inv(k).start()
+
+    barrier = pltpu.get_barrier_semaphore()
+
+    def device(d):
+        o = lax.rem(me + d, devices)
+        return o, {"rows": o // C, "cols": lax.rem(o, C)}
+
+    def greet(d, carry):
+        pl.semaphore_signal(barrier, inc=1, device_id=device(d)[1], device_id_type=MESH)
+        return carry
+
+    lax.fori_loop(1, devices, greet, 0)
+    RC = 128
+
+    def choose(q, carry):
+        rows = pl.ds(pl.multiple_of(q * RC, RC), RC)
+        ids = q * RC + lax.broadcasted_iota(jnp.int32, (RC, select.shape[1]), 0)
+        select[rows, :] = jnp.where(ids == target[...], 1.0, 0.0).astype(jnp.bfloat16)
+        return carry
+
+    lax.fori_loop(0, slots // RC, choose, 0)
+    pl.semaphore_wait(barrier, devices - 1)
+
+    def remote(src, dst, ss, rs, where):
+        return pltpu.make_async_remote_copy(src_ref=src, dst_ref=dst, send_sem=ss, recv_sem=rs,
+                                            device_id=where, device_id_type=MESH)
+
+    def inner_copy(s):
+        return remote(sbuf.at[s], recv_a.at[s], s_sem.at[s], a_sem.at[s], {"rows": inner})
+
+    def swap_copy(s):
+        return remote(sbuf.at[s], xbuf.at[s], s_sem.at[s], x_sem.at[s], {"rows": inner})
+
+    def back_copy(s):
+        return remote(resid.at[s], resid.at[s], bs_sem.at[s], b_sem.at[s], {"rows": outer_safe})
+
+    def pair_copy(s):
+        return remote(pair_s.at[s], pair_r.at[s], ps_sem.at[s], pr_sem.at[s], {"cols": partner})
+
+    def rs_copy(s, d):
+        rows, lanes = share(0, lax.rem(m + d, M))
+        return remote(rs_s.at[s, rows, lanes], rs_r.at[s, d - 1], rss_sem.at[s, d - 1], rsr_sem.at[s, d - 1],
+                      {"cols": peer(d)})
+
+    def ag_copy(s, k, p, d):
+        rows, lanes = share(p * N + h * HALF, m)
+        return remote(xt.at[k, rows, lanes], xt.at[k, rows, lanes], ags_sem.at[s, d - 1], agr_sem.at[s, d - 1],
+                      {"cols": peer(d)})
+
+    def fwd_copy(s, k, p):
+        rows = pl.ds(pl.multiple_of(p * N + h * HALF, HALF), HALF)
+        return remote(xt.at[k, rows], xt.at[k, rows], fs_sem.at[s], fr_sem.at[s], {"cols": partner})
+
+    def half_copy(s, p):
+        rows = pl.ds(pl.multiple_of(p * N + h * HALF, HALF), HALF)
+        lanes = pl.ds(pl.multiple_of(partner * LB, LB), LB)
+        return remote(xt.at[0, rows, lanes], xt.at[0, rows, lanes], fs_sem.at[s], fr_sem.at[s], {"cols": partner})
+
+    def section(rows):
+        return pl.ds(pl.multiple_of(rows * most, most), most)
+
+    def send_copy(g, d):
+        o, where = device(d)
+        return remote(pack.at[g, section(o)], recv.at[g, section(me)], ks_sem.at[g], kr_sem.at[g], where)
+
+    def out_copy(g):
+        return pltpu.make_async_copy(recv.at[g], out.at[:, pl.ds(pl.multiple_of(g * GW, GW), GW)], o_sem.at[g])
+
+    def split(i):
+        k = NB - 1 - i // PC
+        return k, lax.rem(i, PC), lax.rem(i, S)
+
+    def piece(p):
+        return pl.ds(pl.multiple_of(p * N, N), N)
+
+    def first(i):
+        k, p, s = split(i)
+
+        @pl.when(i >= PC)
+        def _():
+            kb, pb, sb = split(i - PC)
+            fwd_copy(sb, kb, pb).wait_recv()
+
+        @pl.when(p == 0)
+        def _():
+            load_pend(k).wait()
+
+        @pl.when(i == PC)
+        def _():
+            load_lower.wait()
+
+        part[p] = pend[k, piece(p), :]
+
+        def add(j, carry):
+            part[p] += jnp.dot(xt[j, piece(p), :], lower[j * (j - 1) // 2 + k],
+                               preferred_element_type=jnp.float32)
+            return carry
+
+        lax.fori_loop(k + 1, NB, add, 0)
+
+        @pl.when(edge)
+        def _():
+            sbuf[s] = part[p].astype(jnp.bfloat16)
+            inner_copy(s).start()
+
+    def second(i):
+        k, p, s = split(i)
+
+        @pl.when(jnp.logical_not(edge))
+        def _():
+            inner_copy(s).wait_recv()
+            part[p] += recv_a[s].astype(jnp.float32)
+            sbuf[s] = part[p].astype(jnp.bfloat16)
+
+            @pl.when(mid)
+            def _():
+                swap_copy(s).start()
+
+            @pl.when(jnp.logical_not(mid))
+            def _():
+                inner_copy(s).start()
+
+    def third(i):
+        k, p, s = split(i)
+
+        @pl.when(mid)
+        def _():
+            swap_copy(s).wait_recv()
+            resid[s] = (-(part[p] + xbuf[s].astype(jnp.float32))).astype(jnp.bfloat16)
+
+        @pl.when(jnp.logical_not(mid))
+        def _():
+            back_copy(s).wait_recv()
+
+        @pl.when(jnp.logical_not(edge))
+        def _():
+            back_copy(s).start()
+
+        @pl.when(p == 0)
+        def _():
+            load_inv(k).wait()
+
+        qbuf[p] = jnp.dot(resid[s], inv[k], preferred_element_type=jnp.float32)
+        theirs = pl.ds(pl.multiple_of((1 - h) * HALF, HALF), HALF)
+        pair_s[s] = qbuf[p, theirs, :].astype(jnp.bfloat16)
+        pair_copy(s).start()
+
+    def fourth(i):
+        k, p, s = split(i)
+        pair_copy(s).wait_recv()
+        mine = pl.ds(pl.multiple_of(h * HALF, HALF), HALF)
+        both = qbuf[p, mine, :] + pair_r[s].astype(jnp.float32)
+        qbuf[p, mine, :] = both
+        rs_s[s] = both.astype(jnp.bfloat16)
+        for d in range(1, M):
+            rs_copy(s, d).start()
+
+    def fifth(i):
+        k, p, s = split(i)
+        rows, lanes = share(h * HALF, m)
+        total = qbuf[p, rows, lanes]
+        for d in range(1, M):
+            rs_copy(s, d).wait_recv()
+        for d in range(1, M):
+            total = total + rs_r[s, d - 1].astype(jnp.float32)
+        rows, lanes = share(p * N + h * HALF, m)
+        xt[k, rows, lanes] = total.astype(jnp.bfloat16)
+
+        @pl.when(k > 0)
+        def _():
+            for d in range(1, M):
+                ag_copy(s, k, p, d).start()
+
+        @pl.when(k == 0)
+        def _():
+            half_copy(s, p).start()
+
+    def sixth(i):
+        k, p, s = split(i)
+
+        @pl.when(k > 0)
+        def _():
+            for d in range(1, M):
+                ag_copy(s, k, p, d).wait_recv()
+            fwd_copy(s, k, p).start()
+
+    def seventh(i):
+        k, p, s = split(i)
+
+        @pl.when(k == 0)
+        def _():
+            half_copy(s, p).wait_recv()
+
+        @pl.when(jnp.logical_and(k == 0, lax.rem(p, PG) == PG - 1))
+        def _():
+            g = p // PG
+            rows = pl.ds(pl.multiple_of(g * GW, GW), GW)
+            lanes = pl.ds(pl.multiple_of(c * LB, LB), LB)
+            for b in range(NB):
+                own[:, b * LB:(b + 1) * LB] = xt[b, rows, lanes]
+
+            def fill(q, carry):
+                part_rows = pl.ds(pl.multiple_of(q * RC, RC), RC)
+                pack[g, part_rows, :] = lax.dot_general(
+                    select[part_rows, :], own[...], (((1,), (1,)), ((), ())), preferred_element_type=jnp.float32
+                ).astype(jnp.bfloat16)
+                return carry
+
+            lax.fori_loop(0, slots // RC, fill, 0)
+
+            def send(d, carry):
+                send_copy(g, d).start()
+                return carry
+
+            lax.fori_loop(1, devices, send, 0)
+            pltpu.make_async_copy(pack.at[g, section(me)], recv.at[g, section(me)], kr_sem.at[g]).start()
+
+    def sends(i):
+        k, p, s = split(i)
+        inner_copy(s).wait_send()
+
+        @pl.when(jnp.logical_not(edge))
+        def _():
+            back_copy(s).wait_send()
+
+        pair_copy(s).wait_send()
+        for d in range(1, M):
+            rs_copy(s, d).wait_send()
+
+        @pl.when(k > 0)
+        def _():
+            for d in range(1, M):
+                ag_copy(s, k, p, d).wait_send()
+            fwd_copy(s, k, p).wait_send()
+
+        @pl.when(k == 0)
+        def _():
+            half_copy(s, p).wait_send()
+
+    mid_lags = [min(lag, LAG_BASE) * (PC - 1) // LAG_BASE for lag in MID_LAGS]
+    end_lags = [min(lag, LAG_BASE) * (PC - 1) // LAG_BASE for lag in END_LAGS]
+    stages = list(zip((first, second, third, fourth, fifth, sixth), mid_lags, end_lags))
+    stages.append((seventh, PC - 1, PC - 1))
+    stages.append((sends, PC + PC // 2, PC + PC // 2))
+
+    def step(t, carry):
+        for stage, mid_lag, end_lag in stages:
+            i = t - jnp.where(mid, mid_lag, end_lag)
+
+            @pl.when(jnp.logical_and(i >= 0, i < items))
+            def _(stage=stage, i=i):
+                stage(i)
+        return carry
+
+    lax.fori_loop(0, items + PC + PC // 2, step, 0)
+
+    def arrive(g, carry):
+        pltpu.make_async_copy(recv.at[g], recv.at[g], kr_sem.at[g]).wait()
+        out_copy(g).start()
+        return carry
+
+    lax.fori_loop(0, G, arrive, 0)
+
+    def finish(g, carry):
+        sent = pack.at[g, pl.ds(0, slots - most)]
+        pltpu.make_async_copy(sent, sent, ks_sem.at[g]).wait()
+        out_copy(g).wait()
+        return carry
+
+    lax.fori_loop(0, G, finish, 0)
+
+
+def fused(pend, lower, inv, target, R, C, most):
+    NB, sources, width = pend.shape
+    depth = inv.shape[2]
+    devices = R * C
+    N = 8 * C
+    PC = sources // N
+    S = 2 * PC
+    M = C // 2
+    GW = GROUP * N
+    G = sources // GW
+    bf, f32 = jnp.bfloat16, jnp.float32
+    dma = pltpu.SemaphoreType.DMA
+    anywhere = pl.BlockSpec(memory_space=pl.ANY)
+    return pl.pallas_call(
+        functools.partial(fused_kernel, (R, C, NB, N, PC, most)),
+        out_shape=jax.ShapeDtypeStruct((devices * most, sources), bf),
+        in_specs=[anywhere, anywhere, anywhere, pl.BlockSpec(memory_space=pltpu.VMEM)],
+        out_specs=pl.BlockSpec(memory_space=pl.ANY),
+        scratch_shapes=[
+            pltpu.VMEM(pend.shape, f32),
+            pltpu.VMEM(lower.shape, bf),
+            pltpu.VMEM(inv.shape, bf),
+            pltpu.VMEM((NB, sources, depth), bf),
+            pltpu.VMEM((PC, N, width), f32),
+            pltpu.VMEM((PC, N, depth), f32),
+            pltpu.VMEM((S, N, width), bf),
+            pltpu.VMEM((S, N, width), bf),
+            pltpu.VMEM((S, N, width), bf),
+            pltpu.VMEM((S, N, width), bf),
+            pltpu.VMEM((S, N // 2, depth), bf),
+            pltpu.VMEM((S, N // 2, depth), bf),
+            pltpu.VMEM((S, N // 2, depth), bf),
+            pltpu.VMEM((S, M - 1, N // 2, depth // M), bf),
+            dma((S,)), dma((S,)), dma((S,)), dma((S,)), dma((S,)), dma((S,)), dma((S,)),
+            dma((S, M - 1)), dma((S, M - 1)), dma((S, M - 1)), dma((S, M - 1)),
+            dma((S,)), dma((S,)), dma((G,)), dma((NB,)), dma((NB,)), dma,
+            pltpu.VMEM((devices * most, target.shape[1]), bf),
+            pltpu.VMEM((GW, target.shape[1]), bf),
+            pltpu.VMEM((G, devices * most, GW), bf),
+            pltpu.VMEM((G, devices * most, GW), bf),
+            dma((G,)), dma((G,)),
+        ],
+        compiler_params=pltpu.CompilerParams(
+            collective_id=1, has_side_effects=True, vmem_limit_bytes=60 * 1024 * 1024
+        ),
+    )(pend, lower, inv, target)
+
+
 def local(pivot_rhs, bound_sol, border_tiles, lower_tiles, inverse_diag, owner_map):
     R = lax.axis_size("rows")
     C = lax.axis_size("cols")
@@ -320,16 +688,20 @@
     else:
         rhs = jnp.where(row == R // 2 - 1, pivot_rhs.transpose(0, 2, 1), 0.0)
     pend = border.transpose(1, 0, 2) - rhs
-    xt = solve(pend, lower_tiles, inverse_diag, R, C)
-
-    own = xt
-    if xt.shape[2] > per_block:
-        own = lax.dynamic_slice_in_dim(xt, lax.axis_index("cols") * per_block, per_block, axis=2)
     owners = owner_map[0, :, 0]
     onehot = (owners[:, None] == jnp.arange(devices, dtype=jnp.int32)[None, :]).astype(jnp.int32)
     ranks = jnp.cumsum(onehot, axis=0) - onehot
     slots = jnp.sum(ranks * onehot, axis=1)
     target = owners * most + slots
+    pieces = 8 * C
+    if pieces // C < 16 and per_block % 128 == 0 and most % 32 == 0 and sources % (GROUP * pieces) == 0:
+        received = fused(pend, lower_tiles, inverse_diag, target[None, :], R, C, most)
+        return received.astype(jnp.float32)
+    xt = solve(pend, lower_tiles, inverse_diag, R, C)
+
+    own = xt
+    if xt.shape[2] > per_block:
+        own = lax.dynamic_slice_in_dim(xt, lax.axis_index("cols") * per_block, per_block, axis=2)
     select = (jnp.arange(devices * most, dtype=jnp.int32)[:, None] == target[None, :]).astype(jnp.bfloat16)
     select = select.reshape(devices * most, blocks, per_block)
     packed = lax.dot_general(

time: 221 us -> 197 us (0.89)
  blocking collectives: 52.8 us -> 0 us
  Pallas kernels: 133 us -> 161 us
  matrix products: 27 us -> 24.5 us
    all_to_all x1 -> x0, blocking collectives: 52.8 us -> none  [local(): lax.all_to_all(packed.reshape(devices, most, sources), ('rows', 'cols'),...]
    pallas_call x1, Pallas kernels: 133 us -> 161 us  [fused(): pl.pallas_call(functools.partial(fused_kernel, (R, C, NB, N, PC, most)),...]
    dot_general x1 -> x0, matrix products: 2.51 us -> none  [local(): lax.dot_general(select, own, (((1, 2), (0, 2)), ((), ())), preferred_elem...]
where the time goes in v1:
time: 197 us; the launch traced here: 196 us
  Pallas kernels  161 us (82%)
  matrix products  24.5 us (12%)
  other arithmetic  5.99 us (3%)
  local copies, waits for them, and re-layouts  3.77 us (2%)
    pallas_call x1, Pallas kernels, fused(): pl.pallas_call(functools.partial(fused_kernel, (R, C, NB, N, PC, most)),...  161 us
    dot_general x1, matrix products, local(): lax.dot_general(bound_sol, border_tiles, (((0,), (0,)), ((), ())), prefer...  24.5 us
    convert_element_type x1, other arithmetic, local(): return received.astype(jnp.float32)  4.07 us

profile of v1, /device:TPU:0, one launch (start us, length us, event | category | flops | bytes accessed | tf_op | source)
XLA Modules:
  0.0 195.5 jit_solution(7331534447108453823)
XLA Ops:
  0.0 1.7 dynamic-slice_bitcast_fusion
  1.7 1.8 copy.11
  3.6 0.0 copy-start
  3.6 24.5 %bitcast_subtract_fusion.pend_in = f32[4,1024,512]{2,1,0:T(8,128)} fusion(f32[1024,512]{1,0:T(8,128)} %copy.11, pred[4]{0:T(512)(128)(4,1)S(1)} %iota_compare_fusion.2, bf16[4096,4,512]{2,1,0:T(4,128)(2,1)} %param.8, bf16[4096,1024]{1,0:T(8,128)(2,1)} %param.7), kind=kOutput, calls=%fused_computation.2 | convolution fusion | flops 17184063488 | bytes 35651588 | tf_op jit(solution)/shard_map/dot_general | solution.py:679
  28.0 0.0 copy-done
  28.1 1.2 reduce-window.6
  29.2 0.2 slice_reduce_fusion
  29.5 0.1 fusion.5
  29.6 0.6 bitcast_add_fusion.target
  30.2 161.3 %shard_map.64 = bf16[1024,1024]{1,0:T(8,128)(2,1)} custom-call(f32[4,1024,512]{2,1,0:T(8,128)} %bitcast_subtract_fusion.pend_in, bf16[6,1024,512]{2,1,0:T(8,128)(2,1)} %lower_in.1, bf16[4,512,1024]{2,1,0:T(8,128)(2,1)} %inv_in.1, s32[1,512]{1,0:T(1,128)} %bitcast_add_fusion.target), custom_call_target="tpu_custom_call" | custom-call | tf_op jit(solution)/shard_map/pallas_call | solution.py:636
  191.5 4.1 %convert_element_type.12 = f32[1024,1024]{1,0:T(8,128)} convert(bf16[1024,1024]{1,0:T(8,128)(2,1)} %shard_map.64) | non-fusion elementwise | flops 1048576 | bytes 6291456 | tf_op jit(solution)/shard_map/convert_element_type | solution.py:699
  (4 shorter events, 0.1 us)
Async XLA Ops:
  3.6 24.5 %copy-start = (s32[1,512,1]{1,2,0:T(1,128)S(1)}, s32[1,512,1]{1,2,0:T(1,128)}, u32[]{:S(2)}) copy-start(s32[1,512,1]{1,2,0:T(1,128)} %param.11) | copy-start | bytes 6148

commit v2 on v1

--- a/solution.py
+++ b/solution.py
@@ -8,10 +8,13 @@
 from jax.sharding import PartitionSpec as P
 
 MESH = pl.DeviceIdType.MESH
-MID_LAGS = (0, 3, 6, 9, 11, 14)
-END_LAGS = (0, 0, 8, 10, 12, 14)
+MID_LAGS = (0, 3, 6, 8, 11, 14)
+END_LAGS = (0, 0, 9, 10, 12, 14)
 LAG_BASE = 15
 GROUP = 4
+RAW = 6
+RAW_ROWS = 256
+VMEM_BYTES = 63 * 1024 * 1024 + 512 * 1024
 
 
 def solve_kernel(dims, pend_in, lower_in, inv_in, out, pend, lower, inv, xt, part, qbuf, sbuf, recv_a, xbuf, resid,
@@ -301,11 +304,11 @@
     )(pend, lower, inv)
 
 
-def fused_kernel(dims, pend_in, lower_in, inv_in, target, out, pend, lower, inv, xt, part, qbuf, sbuf, recv_a, xbuf, resid,
-                 pair_s, pair_r, rs_s, rs_r, s_sem, a_sem, x_sem, b_sem, bs_sem, ps_sem, pr_sem,
-                 rss_sem, rsr_sem, ags_sem, agr_sem, fs_sem, fr_sem, o_sem, pl_sem, il_sem, ll_sem,
-                 select, own, pack, recv, ks_sem, kr_sem):
-    R, C, NB, N, PC, most = dims
+def fused_kernel(dims, rhs_in, bound_in, border_in, lower_in, inv_in, owners, out, tiles, raw, bound, pend, rhs, inv, xt,
+                 part, qbuf, sbuf, recv_a, xbuf, resid, pair_s, pair_r, rs_s, rs_r, select, own, pack, recv,
+                 s_sem, a_sem, x_sem, b_sem, bs_sem, ps_sem, pr_sem, rss_sem, rsr_sem, ags_sem, agr_sem, fs_sem, fr_sem,
+                 o_sem, raw_sem, bd_sem, rhs_sem, il_sem, ll_sem, ks_sem, kr_sem):
+    R, C, NB, N, PC, S, most = dims
     devices = R * C
     M = C // 2
     HALF = N // 2
@@ -314,7 +317,23 @@
     LB = depth // C
     G, slots, GW = pack.shape
     PG = GW // N
-    S = 2 * PC
+    PB = part.shape[0]
+    QB = qbuf.shape[0]
+    NR, RB = raw.shape[:2]
+    QK = bound.shape[1] // depth
+    BW = pend.shape[1]
+    GB = PC // QK
+    chunks = NB * GB
+    blocks_raw = bound.shape[1] // RB
+    late = []
+    for earlier in range(NB - 2, -1, -1):
+        late += [(later, earlier) for later in range(earlier + 1, NB)]
+    late_unit = {}
+    for n, (later, earlier) in enumerate(late):
+        unit = NB * QK if n == 0 else (NB - 1) * QK + n - 1
+        if n > QK:
+            unit = NB * QK + n - QK
+        late_unit[later * (later - 1) // 2 + earlier] = unit
     items = NB * PC
     z = lax.axis_index("rows")
     c = lax.axis_index("cols")
@@ -335,19 +354,87 @@
     def share(base, q):
         return pl.ds(pl.multiple_of(base, HALF), HALF), pl.ds(pl.multiple_of(q * LW, LW), LW)
 
-    def load_pend(k):
-        return pltpu.make_async_copy(pend_in.at[k], pend.at[k], pl_sem.at[k])
-
     def load_inv(k):
         return pltpu.make_async_copy(inv_in.at[k], inv.at[k], il_sem.at[k])
 
-    load_lower = pltpu.make_async_copy(lower_in, lower, ll_sem)
-    load_pend(NB - 1).start()
+    def load_lower(n):
+        pair = late[n][0] * (late[n][0] - 1) // 2 + late[n][1]
+        return pltpu.make_async_copy(lower_in.at[pair], tiles.at[late_unit[pair]], ll_sem.at[n])
+
+    def load_raw(e):
+        pair = NB // 2 - 1 - e // blocks_raw
+        rows = pl.ds(pl.multiple_of(lax.rem(e, blocks_raw) * RB, RB), RB)
+        slot = lax.rem(e, NR)
+        return pltpu.make_async_copy(border_in.at[rows, pl.ds(2 * pair, 2), :], raw.at[slot], raw_sem.at[slot])
+
+    def load_bound(q):
+        return pltpu.make_async_copy(bound_in.at[pl.ds(q * depth, depth)], xt.at[q], bd_sem.at[q])
+
+    def load_rhs(g):
+        lanes = pl.ds(pl.multiple_of(g * BW, BW), BW)
+        slot = lax.rem(g, 2)
+        return pltpu.make_async_copy(rhs_in.at[z, :, lanes], rhs.at[slot], rhs_sem.at[slot])
+
+    def untangle(e):
+        pair = NB // 2 - 1 - e // blocks_raw
+        start = lax.rem(e, blocks_raw) * RB
+        rows = pl.ds(pl.multiple_of(lax.rem(start, depth), RB), RB)
+        load_raw(e).wait()
+        both = jnp.swapaxes(raw[lax.rem(e, NR)], 0, 1)
+        for b in range(2):
+            tiles[(2 * pair + b) * QK + start // depth, rows, :] = both[b]
+
+        @pl.when(e + NR < NB // 2 * blocks_raw)
+        def _():
+            load_raw(e + NR).start()
+
+    def turn(g, q):
+        rows = pl.ds(pl.multiple_of(g * BW, BW), BW)
+        lanes = pl.ds(pl.multiple_of(q * depth, depth), depth)
+        bound[rows, lanes] = xt[q, :, rows].T
+
+    def border(j, half):
+        k = NB - 1 - j // GB
+        g = lax.rem(j, GB)
+        slot = lax.rem(j, 2)
+        rows = pl.ds(pl.multiple_of(g * BW, BW), BW)
+        width = pend.shape[2]
+        lanes = pl.ds(pl.multiple_of(half * (width // 2), width // 2), width // 2)
+        block = tiles[pl.ds(k * QK, QK), :, lanes].reshape(QK * depth, width // 2)
+        pend[slot, :, lanes] = jnp.dot(bound[rows, :], block, preferred_element_type=jnp.float32)
+
+        @pl.when(jnp.logical_and(half == 1, k == z))
+        def _():
+            load_rhs(g).wait()
+            pend[slot] -= rhs[lax.rem(g, 2)].T
+
+            @pl.when(g + 2 < GB)
+            def _():
+                load_rhs(g + 2).start()
+
+    def unit_of(pair):
+        unit = late_unit[0]
+        for n in range(1, len(late)):
+            unit = jnp.where(pair == n, late_unit[n], unit)
+        return unit
+
+    def ahead(j, later):
+        k = NB - 1 - j // GB
+        rows = pl.ds(pl.multiple_of(lax.rem(j, GB) * BW, BW), BW)
+        pend[lax.rem(j, 2)] += jnp.dot(
+            xt[later, rows, :], tiles[unit_of(later * (later - 1) // 2 + k)], preferred_element_type=jnp.float32
+        )
+
+    def first_raw(e, carry):
+        load_raw(e).start()
+        return carry
+
+    lax.fori_loop(0, NR, first_raw, 0)
+    for q in range(QK - 1, -1, -1):
+        load_bound(q).start()
+    load_rhs(0).start()
+    load_rhs(1).start()
     load_inv(NB - 1).start()
-    load_lower.start()
-    for k in range(NB - 2, -1, -1):
-        load_pend(k).start()
-        load_inv(k).start()
 
     barrier = pltpu.get_barrier_semaphore()
 
@@ -361,14 +448,44 @@
 
     lax.fori_loop(1, devices, greet, 0)
     RC = 128
+    FC = slots // 2
+
+    wide = select.shape[1]
+    names = owners[...].astype(jnp.float32)
+    ranks = jnp.zeros((1, wide), jnp.float32)
+    for q in range(0, wide, RC):
+        down = q + lax.broadcasted_iota(jnp.int32, (RC, wide), 0)
+        over = lax.broadcasted_iota(jnp.int32, (RC, wide), 1)
+        column = jnp.sum(jnp.where(down == over, names, 0.0), axis=1, keepdims=True)
+        same = jnp.logical_and(column == names, down < over)
+        ranks = ranks + jnp.sum(jnp.where(same, 1.0, 0.0), axis=0, keepdims=True)
+    target = (names * most + ranks).astype(jnp.int32)
 
     def choose(q, carry):
         rows = pl.ds(pl.multiple_of(q * RC, RC), RC)
-        ids = q * RC + lax.broadcasted_iota(jnp.int32, (RC, select.shape[1]), 0)
-        select[rows, :] = jnp.where(ids == target[...], 1.0, 0.0).astype(jnp.bfloat16)
+        ids = q * RC + lax.broadcasted_iota(jnp.int32, (RC, wide), 0)
+        select[rows, :] = jnp.where(ids == target, 1.0, 0.0).astype(jnp.bfloat16)
         return carry
 
     lax.fori_loop(0, slots // RC, choose, 0)
+
+    def first_half(e, carry):
+        untangle(e)
+        return carry
+
+    lax.fori_loop(0, blocks_raw, first_half, 0)
+    for b in range(NB - 2, -1, -1):
+        load_inv(b).start()
+    load_lower(0).start()
+    load_bound(QK - 1).wait()
+    for g in range(GB):
+        turn(g, QK - 1)
+    for q in range(QK - 1):
+        load_bound(q).wait()
+        turn(0, q)
+        turn(1, q)
+    border(0, 0)
+    border(0, 1)
     pl.semaphore_wait(barrier, devices - 1)
 
     def remote(src, dst, ss, rs, where):
@@ -389,12 +506,15 @@
 
     def rs_copy(s, d):
         rows, lanes = share(0, lax.rem(m + d, M))
-        return remote(rs_s.at[s, rows, lanes], rs_r.at[s, d - 1], rss_sem.at[s, d - 1], rsr_sem.at[s, d - 1],
+        return remote(rs_s.at[s, rows, lanes], rs_r.at[s, d - 1], rss_sem.at[s], rsr_sem.at[s],
                       {"cols": peer(d)})
+
+    def all_of(s, sem):
+        return pltpu.make_async_copy(rs_r.at[s], rs_r.at[s], sem.at[s])
 
     def ag_copy(s, k, p, d):
         rows, lanes = share(p * N + h * HALF, m)
-        return remote(xt.at[k, rows, lanes], xt.at[k, rows, lanes], ags_sem.at[s, d - 1], agr_sem.at[s, d - 1],
+        return remote(xt.at[k, rows, lanes], xt.at[k, rows, lanes], ags_sem.at[s], agr_sem.at[s],
                       {"cols": peer(d)})
 
     def fwd_copy(s, k, p):
@@ -431,86 +551,95 @@
             kb, pb, sb = split(i - PC)
             fwd_copy(sb, kb, pb).wait_recv()
 
+        @pl.when(i == PC)
+        def _():
+            load_lower(0).wait()
+
+        @pl.when(i == 2 * PC - QK)
+        def _():
+            for n in range(1, len(late)):
+                load_lower(n).wait()
+
+        a = lax.rem(i, PB)
+        ready = pl.ds(pl.multiple_of(lax.rem(i, QK) * N, N), N)
+
+        def hold(value):
+            @pl.when(edge)
+            def _():
+                sbuf[s] = value.astype(jnp.bfloat16)
+                inner_copy(s).start()
+
+            @pl.when(jnp.logical_not(edge))
+            def _():
+                part[a] = value
+
+        @pl.when(i < PC)
+        def _():
+            hold(pend[lax.rem(i // QK, 2), ready, :])
+
+        @pl.when(i >= PC)
+        def _():
+            j = k + 1
+            hold(pend[lax.rem(i // QK, 2), ready, :] + jnp.dot(
+                xt[j, piece(p), :], tiles[unit_of(j * (j - 1) // 2 + k)], preferred_element_type=jnp.float32
+            ))
+
+    def second(i):
+        k, p, s = split(i)
+
+        @pl.when(jnp.logical_not(edge))
+        def _():
+            a = lax.rem(i, PB)
+            inner_copy(s).wait_recv()
+            both = part[a] + recv_a[s].astype(jnp.float32)
+            part[a] = both
+            sbuf[s] = both.astype(jnp.bfloat16)
+
+            @pl.when(mid)
+            def _():
+                swap_copy(s).start()
+
+            @pl.when(jnp.logical_not(mid))
+            def _():
+                inner_copy(s).start()
+
+    def third(i):
+        k, p, s = split(i)
+
+        @pl.when(mid)
+        def _():
+            swap_copy(s).wait_recv()
+            resid[s] = (-(part[lax.rem(i, PB)] + xbuf[s].astype(jnp.float32))).astype(jnp.bfloat16)
+
+        @pl.when(jnp.logical_not(mid))
+        def _():
+            back_copy(s).wait_recv()
+
+        @pl.when(jnp.logical_not(edge))
+        def _():
+            back_copy(s).start()
+
         @pl.when(p == 0)
         def _():
-            load_pend(k).wait()
-
-        @pl.when(i == PC)
-        def _():
-            load_lower.wait()
-
-        part[p] = pend[k, piece(p), :]
-
-        def add(j, carry):
-            part[p] += jnp.dot(xt[j, piece(p), :], lower[j * (j - 1) // 2 + k],
-                               preferred_element_type=jnp.float32)
-            return carry
-
-        lax.fori_loop(k + 1, NB, add, 0)
-
-        @pl.when(edge)
-        def _():
-            sbuf[s] = part[p].astype(jnp.bfloat16)
-            inner_copy(s).start()
-
-    def second(i):
-        k, p, s = split(i)
-
-        @pl.when(jnp.logical_not(edge))
-        def _():
-            inner_copy(s).wait_recv()
-            part[p] += recv_a[s].astype(jnp.float32)
-            sbuf[s] = part[p].astype(jnp.bfloat16)
-
-            @pl.when(mid)
-            def _():
-                swap_copy(s).start()
-
-            @pl.when(jnp.logical_not(mid))
-            def _():
-                inner_copy(s).start()
-
-    def third(i):
-        k, p, s = split(i)
-
-        @pl.when(mid)
-        def _():
-            swap_copy(s).wait_recv()
-            resid[s] = (-(part[p] + xbuf[s].astype(jnp.float32))).astype(jnp.bfloat16)
-
-        @pl.when(jnp.logical_not(mid))
-        def _():
-            back_copy(s).wait_recv()
-
-        @pl.when(jnp.logical_not(edge))
-        def _():
-            back_copy(s).start()
-
-        @pl.when(p == 0)
-        def _():
             load_inv(k).wait()
 
-        qbuf[p] = jnp.dot(resid[s], inv[k], preferred_element_type=jnp.float32)
-        theirs = pl.ds(pl.multiple_of((1 - h) * HALF, HALF), HALF)
-        pair_s[s] = qbuf[p, theirs, :].astype(jnp.bfloat16)
+        terms = jnp.dot(resid[s], inv[k], preferred_element_type=jnp.float32)
+        pair_s[s] = jnp.where(h == 0, terms[HALF:], terms[:HALF]).astype(jnp.bfloat16)
         pair_copy(s).start()
+        qbuf[lax.rem(i, QB)] = jnp.where(h == 0, terms[:HALF], terms[HALF:])
 
     def fourth(i):
         k, p, s = split(i)
         pair_copy(s).wait_recv()
-        mine = pl.ds(pl.multiple_of(h * HALF, HALF), HALF)
-        both = qbuf[p, mine, :] + pair_r[s].astype(jnp.float32)
-        qbuf[p, mine, :] = both
-        rs_s[s] = both.astype(jnp.bfloat16)
+        rs_s[s] = (qbuf[lax.rem(i, QB)] + pair_r[s].astype(jnp.float32)).astype(jnp.bfloat16)
         for d in range(1, M):
             rs_copy(s, d).start()
 
     def fifth(i):
         k, p, s = split(i)
-        rows, lanes = share(h * HALF, m)
-        total = qbuf[p, rows, lanes]
-        for d in range(1, M):
-            rs_copy(s, d).wait_recv()
+        lanes = share(0, m)[1]
+        total = qbuf[lax.rem(i, QB), :, lanes] + pair_r[s, :, lanes].astype(jnp.float32)
+        all_of(s, rsr_sem).wait()
         for d in range(1, M):
             total = total + rs_r[s, d - 1].astype(jnp.float32)
         rows, lanes = share(p * N + h * HALF, m)
@@ -530,8 +659,7 @@
 
         @pl.when(k > 0)
         def _():
-            for d in range(1, M):
-                ag_copy(s, k, p, d).wait_recv()
+            all_of(s, agr_sem).wait()
             fwd_copy(s, k, p).start()
 
     def seventh(i):
@@ -550,13 +678,13 @@
                 own[:, b * LB:(b + 1) * LB] = xt[b, rows, lanes]
 
             def fill(q, carry):
-                part_rows = pl.ds(pl.multiple_of(q * RC, RC), RC)
+                part_rows = pl.ds(pl.multiple_of(q * FC, FC), FC)
                 pack[g, part_rows, :] = lax.dot_general(
                     select[part_rows, :], own[...], (((1,), (1,)), ((), ())), preferred_element_type=jnp.float32
                 ).astype(jnp.bfloat16)
                 return carry
 
-            lax.fori_loop(0, slots // RC, fill, 0)
+            lax.fori_loop(0, slots // FC, fill, 0)
 
             def send(d, carry):
                 send_copy(g, d).start()
@@ -574,13 +702,11 @@
             back_copy(s).wait_send()
 
         pair_copy(s).wait_send()
-        for d in range(1, M):
-            rs_copy(s, d).wait_send()
+        all_of(s, rss_sem).wait()
 
         @pl.when(k > 0)
         def _():
-            for d in range(1, M):
-                ag_copy(s, k, p, d).wait_send()
+            all_of(s, ags_sem).wait()
             fwd_copy(s, k, p).wait_send()
 
         @pl.when(k == 0)
@@ -591,7 +717,7 @@
     end_lags = [min(lag, LAG_BASE) * (PC - 1) // LAG_BASE for lag in END_LAGS]
     stages = list(zip((first, second, third, fourth, fifth, sixth), mid_lags, end_lags))
     stages.append((seventh, PC - 1, PC - 1))
-    stages.append((sends, PC + PC // 2, PC + PC // 2))
+    stages.append((sends, S - 1, S - 1))
 
     def step(t, carry):
         for stage, mid_lag, end_lag in stages:
@@ -600,9 +726,36 @@
             @pl.when(jnp.logical_and(i >= 0, i < items))
             def _(stage=stage, i=i):
                 stage(i)
+
+        @pl.when(t < blocks_raw)
+        def _():
+            untangle(blocks_raw + t)
+
+        @pl.when(t < QK * (chunks - 1))
+        def _():
+            j, q = t // QK + 1, lax.rem(t, QK)
+
+            k = NB - 1 - j // GB
+
+            @pl.when(q < 2)
+            def _():
+                border(j, q)
+
+            @pl.when(jnp.logical_and(q >= 2, q < NB - k))
+            def _():
+                ahead(j, k + q)
+
+            @pl.when(jnp.logical_and(j + 1 < GB, q > 0))
+            def _():
+                turn(j + 1, q - 1)
+
+        @pl.when(t == QK * (GB - 1))
+        def _():
+            for n in range(1, len(late)):
+                load_lower(n).start()
         return carry
 
-    lax.fori_loop(0, items + PC + PC // 2, step, 0)
+    lax.fori_loop(0, items + S - 1, step, 0)
 
     def arrive(g, carry):
         pltpu.make_async_copy(recv.at[g], recv.at[g], kr_sem.at[g]).wait()
@@ -620,31 +773,38 @@
     lax.fori_loop(0, G, finish, 0)
 
 
-def fused(pend, lower, inv, target, R, C, most):
-    NB, sources, width = pend.shape
+def fused(rhs, bound, border, lower, inv, owners, R, C, most):
+    NB, width, sources = rhs.shape
     depth = inv.shape[2]
     devices = R * C
     N = 8 * C
     PC = sources // N
-    S = 2 * PC
+    S = PC + 4
     M = C // 2
     GW = GROUP * N
     G = sources // GW
+    QK = bound.shape[0] // depth
+    pairs = lower.shape[0]
+    PB = max(MID_LAGS[2], END_LAGS[2]) + 2
+    QB = max(MID_LAGS[4] - MID_LAGS[2], END_LAGS[4] - END_LAGS[2]) + 2
     bf, f32 = jnp.bfloat16, jnp.float32
     dma = pltpu.SemaphoreType.DMA
     anywhere = pl.BlockSpec(memory_space=pl.ANY)
     return pl.pallas_call(
-        functools.partial(fused_kernel, (R, C, NB, N, PC, most)),
+        functools.partial(fused_kernel, (R, C, NB, N, PC, S, most)),
         out_shape=jax.ShapeDtypeStruct((devices * most, sources), bf),
-        in_specs=[anywhere, anywhere, anywhere, pl.BlockSpec(memory_space=pltpu.VMEM)],
+        in_specs=[anywhere] * 5 + [pl.BlockSpec(memory_space=pltpu.VMEM)],
         out_specs=pl.BlockSpec(memory_space=pl.ANY),
         scratch_shapes=[
-            pltpu.VMEM(pend.shape, f32),
-            pltpu.VMEM(lower.shape, bf),
+            pltpu.VMEM((NB * QK + 1 + max(0, pairs - 1 - QK), depth, width), bf),
+            pltpu.VMEM((RAW, RAW_ROWS, 2, width), bf),
+            pltpu.VMEM((sources, bound.shape[0]), bf),
+            pltpu.VMEM((2, QK * N, width), f32),
+            pltpu.VMEM((2, width, QK * N), f32),
             pltpu.VMEM(inv.shape, bf),
             pltpu.VMEM((NB, sources, depth), bf),
-            pltpu.VMEM((PC, N, width), f32),
-            pltpu.VMEM((PC, N, depth), f32),
+            pltpu.VMEM((PB, N, width), f32),
+            pltpu.VMEM((QB, N // 2, depth), f32),
             pltpu.VMEM((S, N, width), bf),
             pltpu.VMEM((S, N, width), bf),
             pltpu.VMEM((S, N, width), bf),
@@ -653,19 +813,19 @@
             pltpu.VMEM((S, N // 2, depth), bf),
             pltpu.VMEM((S, N // 2, depth), bf),
             pltpu.VMEM((S, M - 1, N // 2, depth // M), bf),
-            dma((S,)), dma((S,)), dma((S,)), dma((S,)), dma((S,)), dma((S,)), dma((S,)),
-            dma((S, M - 1)), dma((S, M - 1)), dma((S, M - 1)), dma((S, M - 1)),
-            dma((S,)), dma((S,)), dma((G,)), dma((NB,)), dma((NB,)), dma,
-            pltpu.VMEM((devices * most, target.shape[1]), bf),
-            pltpu.VMEM((GW, target.shape[1]), bf),
+            pltpu.VMEM((devices * most, owners.shape[1]), bf),
+            pltpu.VMEM((GW, owners.shape[1]), bf),
             pltpu.VMEM((G, devices * most, GW), bf),
             pltpu.VMEM((G, devices * most, GW), bf),
+            dma((S,)), dma((S,)), dma((S,)), dma((S,)), dma((S,)), dma((S,)), dma((S,)),
+            dma((S,)), dma((S,)), dma((S,)), dma((S,)),
+            dma((S,)), dma((S,)), dma((G,)), dma((RAW,)), dma((QK,)), dma((2,)), dma((NB,)), dma((pairs,)),
             dma((G,)), dma((G,)),
         ],
         compiler_params=pltpu.CompilerParams(
-            collective_id=1, has_side_effects=True, vmem_limit_bytes=60 * 1024 * 1024
+            collective_id=1, has_side_effects=True, vmem_limit_bytes=VMEM_BYTES
         ),
-    )(pend, lower, inv, target)
+    )(rhs, bound, border, lower, inv, owners)
 
 
 def local(pivot_rhs, bound_sol, border_tiles, lower_tiles, inverse_diag, owner_map):
@@ -676,6 +836,17 @@
     rows_dev = owner_map.shape[1]
     per_block = rows_dev // blocks
     most = max(2, 2 * rows_dev // devices)
+    pieces = 8 * C
+    depth = inverse_diag.shape[2]
+    if (
+        R == blocks == 4 and C >= 4 and depth == sources and depth == per_block * C and bound_sol.shape[0] == 4 * depth
+        and per_block % 128 == 0 and most % 32 == 0 and sources % (4 * pieces) == 0 and sources == 16 * pieces
+        and bound_sol.shape[0] % RAW_ROWS == 0
+    ):
+        received = fused(
+            pivot_rhs, bound_sol, border_tiles, lower_tiles, inverse_diag, owner_map[:, :, 0], R, C, most
+        )
+        return received.astype(jnp.float32)
     border = lax.dot_general(
         bound_sol, border_tiles, (((0,), (0,)), ((), ())), preferred_element_type=jnp.float32
     )
@@ -693,10 +864,6 @@
     ranks = jnp.cumsum(onehot, axis=0) - onehot
     slots = jnp.sum(ranks * onehot, axis=1)
     target = owners * most + slots
-    pieces = 8 * C
-    if pieces // C < 16 and per_block % 128 == 0 and most % 32 == 0 and sources % (GROUP * pieces) == 0:
-        received = fused(pend, lower_tiles, inverse_diag, target[None, :], R, C, most)
-        return received.astype(jnp.float32)
     xt = solve(pend, lower_tiles, inverse_diag, R, C)
 
     own = xt

time: 197 us -> 174 us (0.88)
  matrix products: 24.5 us -> 0 us
  Pallas kernels: 161 us -> 169 us
  local copies, waits for them, and re-layouts: 3.77 us -> 0 us
    dot_general x1 -> x0, matrix products: 24.5 us -> none  [local(): lax.dot_general(bound_sol, border_tiles, (((0,), (0,)), ((), ())), prefer...]
    pallas_call x1, Pallas kernels: 161 us -> 169 us  [fused(): pl.pallas_call(functools.partial(fused_kernel, (R, C, NB, N, PC, S, most)...]
    transpose x2 -> x0, local copies, waits for them, and re-layouts: 3.54 us -> none  [local(): rhs = lax.dynamic_index_in_dim(pivot_rhs, block, 0, keepdims=False).T[None]]
where the time goes in v2:
time: 174 us; the launch traced here: 173 us
  Pallas kernels  169 us (97%)
  other arithmetic  4.07 us (2%)
    pallas_call x1, Pallas kernels, fused(): pl.pallas_call(functools.partial(fused_kernel, (R, C, NB, N, PC, S, most)...  169 us
    convert_element_type x1, other arithmetic, local(): return received.astype(jnp.float32)  4.07 us

profile of v2, /device:TPU:0, one launch (start us, length us, event | category | flops | bytes accessed | tf_op | source)
XLA Modules:
  0.0 172.7 jit_solution(25204529514604240)
XLA Ops:
  0.0 168.6 %shard_map.64 = bf16[1024,1024]{1,0:T(8,128)(2,1)} custom-call(f32[4,512,1024]{2,1,0:T(8,128)} %rhs_in.1, bf16[4096,1024]{1,0:T(8,128)(2,1)} %bound_in.1, bf16[4096,4,512]{2,1,0:T(4,128)(2,1)} %border_in.1, bf16[6,1024,512]{2,1,0:T(8,128)(2,1)} %lower_in.1, bf16[4,512,1024]{2,1,0:T(8,128)(2,1)} %inv_in.1, s32[1,512]{1,0:T(1,128)} %bitcast.1), custom_call_target="tpu_custom_call" | custom-call | tf_op jit(solution)/shard_map/pallas_call | solution.py:793
  168.6 4.1 %convert_element_type.3 = f32[1024,1024]{1,0:T(8,128)} convert(bf16[1024,1024]{1,0:T(8,128)(2,1)} %shard_map.64) | non-fusion elementwise | flops 1048576 | bytes 6291456 | tf_op jit(solution)/shard_map/convert_element_type | solution.py:849

commit v3 on v2

--- a/solution.py
+++ b/solution.py
@@ -13,6 +13,7 @@
 LAG_BASE = 15
 GROUP = 4
 RAW = 6
+PARTS = 8
 RAW_ROWS = 256
 VMEM_BYTES = 63 * 1024 * 1024 + 512 * 1024
 
@@ -418,11 +419,14 @@
             unit = jnp.where(pair == n, late_unit[n], unit)
         return unit
 
-    def ahead(j, later):
+    def ahead(j, half, later):
         k = NB - 1 - j // GB
         rows = pl.ds(pl.multiple_of(lax.rem(j, GB) * BW, BW), BW)
-        pend[lax.rem(j, 2)] += jnp.dot(
-            xt[later, rows, :], tiles[unit_of(later * (later - 1) // 2 + k)], preferred_element_type=jnp.float32
+        width = pend.shape[2]
+        lanes = pl.ds(pl.multiple_of(half * (width // 2), width // 2), width // 2)
+        pend[lax.rem(j, 2), :, lanes] += jnp.dot(
+            xt[later, rows, :], tiles[unit_of(later * (later - 1) // 2 + k), :, lanes],
+            preferred_element_type=jnp.float32,
         )
 
     def first_raw(e, carry):
@@ -430,8 +434,9 @@
         return carry
 
     lax.fori_loop(0, NR, first_raw, 0)
-    for q in range(QK - 1, -1, -1):
-        load_bound(q).start()
+    order = [QK - 1] + list(range(QK - 1))
+    load_bound(order[0]).start()
+    load_bound(order[1]).start()
     load_rhs(0).start()
     load_rhs(1).start()
     load_inv(NB - 1).start()
@@ -473,17 +478,17 @@
         untangle(e)
         return carry
 
-    lax.fori_loop(0, blocks_raw, first_half, 0)
+    stretch = blocks_raw // QK
+    for n in range(QK):
+        lax.fori_loop(n * stretch, (n + 1) * stretch, first_half, 0)
+        if n + 2 < QK:
+            load_bound(order[n + 2]).start()
+        load_bound(order[n]).wait()
+        for g in range(GB if n == 0 else 2):
+            turn(g, order[n])
     for b in range(NB - 2, -1, -1):
         load_inv(b).start()
     load_lower(0).start()
-    load_bound(QK - 1).wait()
-    for g in range(GB):
-        turn(g, QK - 1)
-    for q in range(QK - 1):
-        load_bound(q).wait()
-        turn(0, q)
-        turn(1, q)
     border(0, 0)
     border(0, 1)
     pl.semaphore_wait(barrier, devices - 1)
@@ -719,35 +724,43 @@
     stages.append((seventh, PC - 1, PC - 1))
     stages.append((sends, S - 1, S - 1))
 
+    def fill_in(t):
+        @pl.when(t < blocks_raw)
+        def _():
+            untangle(blocks_raw + t)
+
+        @pl.when(t < QK * (chunks - 1))
+        def _():
+            j, q = t // QK + 1, lax.rem(t, QK)
+
+            k = NB - 1 - j // GB
+
+            @pl.when(lax.rem(q, 2) == 0)
+            def _():
+                border(j, q // 2)
+
+            @pl.when(jnp.logical_and(lax.rem(q, 2) == 1, k + 2 < NB))
+            def _():
+                ahead(j, q // 2, k + 2)
+
+            @pl.when(jnp.logical_and(lax.rem(q, 2) == 1, k + 3 < NB))
+            def _():
+                ahead(j, q // 2, k + 3)
+
+            @pl.when(jnp.logical_and(j + 1 < GB, q > 0))
+            def _():
+                turn(j + 1, q - 1)
+
+
     def step(t, carry):
-        for stage, mid_lag, end_lag in stages:
+        for n, (stage, mid_lag, end_lag) in enumerate(stages):
+            if n == 1:
+                fill_in(t)
             i = t - jnp.where(mid, mid_lag, end_lag)
 
             @pl.when(jnp.logical_and(i >= 0, i < items))
             def _(stage=stage, i=i):
                 stage(i)
-
-        @pl.when(t < blocks_raw)
-        def _():
-            untangle(blocks_raw + t)
-
-        @pl.when(t < QK * (chunks - 1))
-        def _():
-            j, q = t // QK + 1, lax.rem(t, QK)
-
-            k = NB - 1 - j // GB
-
-            @pl.when(q < 2)
-            def _():
-                border(j, q)
-
-            @pl.when(jnp.logical_and(q >= 2, q < NB - k))
-            def _():
-                ahead(j, k + q)
-
-            @pl.when(jnp.logical_and(j + 1 < GB, q > 0))
-            def _():
-                turn(j + 1, q - 1)
 
         @pl.when(t == QK * (GB - 1))
         def _():
@@ -828,6 +841,41 @@
     )(rhs, bound, border, lower, inv, owners)
 
 
+def widen_kernel(source, out, narrow, full, in_sem, out_sem):
+    parts = in_sem.shape[0]
+    rows = source.shape[0] // parts
+
+    def take(n):
+        part = pl.ds(n * rows, rows)
+        return pltpu.make_async_copy(source.at[part], narrow.at[part], in_sem.at[n])
+
+    def give(n):
+        part = pl.ds(n * rows, rows)
+        return pltpu.make_async_copy(full.at[part], out.at[part], out_sem.at[n])
+
+    for n in range(parts):
+        take(n).start()
+    for n in range(parts):
+        take(n).wait()
+        full[n * rows:(n + 1) * rows, :] = narrow[n * rows:(n + 1) * rows, :].astype(jnp.float32)
+        give(n).start()
+    for n in range(parts):
+        give(n).wait()
+
+
+def widen(values):
+    dma = pltpu.SemaphoreType.DMA
+    return pl.pallas_call(
+        widen_kernel,
+        out_shape=jax.ShapeDtypeStruct(values.shape, jnp.float32),
+        in_specs=[pl.BlockSpec(memory_space=pl.ANY)],
+        out_specs=pl.BlockSpec(memory_space=pl.ANY),
+        scratch_shapes=[
+            pltpu.VMEM(values.shape, values.dtype), pltpu.VMEM(values.shape, jnp.float32), dma((PARTS,)), dma((PARTS,)),
+        ],
+    )(values)
+
+
 def local(pivot_rhs, bound_sol, border_tiles, lower_tiles, inverse_diag, owner_map):
     R = lax.axis_size("rows")
     C = lax.axis_size("cols")
@@ -846,7 +894,7 @@
         received = fused(
             pivot_rhs, bound_sol, border_tiles, lower_tiles, inverse_diag, owner_map[:, :, 0], R, C, most
         )
-        return received.astype(jnp.float32)
+        return widen(received)
     border = lax.dot_general(
         bound_sol, border_tiles, (((0,), (0,)), ((), ())), preferred_element_type=jnp.float32
     )

time: 174 us -> 170 us (0.977)
  other arithmetic: 4.07 us -> 0 us
    convert_element_type x1 -> x0, other arithmetic: 4.07 us -> none  [local(): return received.astype(jnp.float32)]
    pallas_call x1, Pallas kernels: 169 us -> 165 us  [fused(): pl.pallas_call(functools.partial(fused_kernel, (R, C, NB, N, PC, S, most)...]
    pallas_call x0 -> x1, Pallas kernels: none -> 3.12 us  [widen(): pl.pallas_call(widen_kernel, out_shape=jax.ShapeDtypeStruct(values.shape,...]
where the time goes in v3:
time: 170 us; the launch traced here: 168 us
  Pallas kernels  168 us (99%)
    pallas_call x1, Pallas kernels, fused(): pl.pallas_call(functools.partial(fused_kernel, (R, C, NB, N, PC, S, most)...  165 us

profile of v3, /device:TPU:0, one launch (start us, length us, event | category | flops | bytes accessed | tf_op | source)
XLA Modules:
  0.0 167.9 jit_solution(13335192035951943688)
XLA Ops:
  0.0 164.8 %shard_map.64.source = bf16[1024,1024]{1,0:T(8,128)(2,1)} custom-call(f32[4,512,1024]{2,1,0:T(8,128)} %rhs_in.1, bf16[4096,1024]{1,0:T(8,128)(2,1)} %bound_in.1, bf16[4096,4,512]{2,1,0:T(4,128)(2,1)} %border_in.1, bf16[6,1024,512]{2,1,0:T(8,128)(2,1)} %lower_in.1, bf16[4,512,1024]{2,1,0:T(8,128)(2,1)} %inv_in.1, s32[1,512]{1,0:T(1,128)} %bitcast.1), custom_call_target="tpu_custom_call" | custom-call | tf_op jit(solution)/shard_map/pallas_call | solution.py:806
  164.8 3.1 %shard_map.65 = f32[1024,1024]{1,0:T(8,128)} custom-call(bf16[1024,1024]{1,0:T(8,128)(2,1)} %shard_map.64.source), custom_call_target="tpu_custom_call" | custom-call | tf_op jit(solution)/shard_map/pallas_call | solution.py:868

commit v4 on v3

--- a/solution.py
+++ b/solution.py
@@ -349,8 +349,13 @@
     partner = c + 1 - 2 * h
     me = z * C + c
 
+    def place(d):
+        if M == 4:
+            return 2 * lax.rem(m // 2 + d // 2, 2) + lax.rem(m + d, 2)
+        return lax.rem(m + d, M)
+
     def peer(d):
-        return 2 * lax.rem(m + d, M) + h
+        return 2 * place(d) + h
 
     def share(base, q):
         return pl.ds(pl.multiple_of(base, HALF), HALF), pl.ds(pl.multiple_of(q * LW, LW), LW)
@@ -510,7 +515,7 @@
         return remote(pair_s.at[s], pair_r.at[s], ps_sem.at[s], pr_sem.at[s], {"cols": partner})
 
     def rs_copy(s, d):
-        rows, lanes = share(0, lax.rem(m + d, M))
+        rows, lanes = share(0, place(d))
         return remote(rs_s.at[s, rows, lanes], rs_r.at[s, d - 1], rss_sem.at[s], rsr_sem.at[s],
                       {"cols": peer(d)})
 
@@ -637,7 +642,7 @@
         k, p, s = split(i)
         pair_copy(s).wait_recv()
         rs_s[s] = (qbuf[lax.rem(i, QB)] + pair_r[s].astype(jnp.float32)).astype(jnp.bfloat16)
-        for d in range(1, M):
+        for d in range(M - 1, 0, -1):
             rs_copy(s, d).start()
 
     def fifth(i):
@@ -652,7 +657,7 @@
 
         @pl.when(k > 0)
         def _():
-            for d in range(1, M):
+            for d in range(M - 1, 0, -1):
                 ag_copy(s, k, p, d).start()
 
         @pl.when(k == 0)

time: 170 us -> 167 us (0.982)
  Pallas kernels: 168 us -> 166 us
    pallas_call x1, Pallas kernels: 165 us -> 163 us  [fused(): pl.pallas_call(functools.partial(fused_kernel, (R, C, NB, N, PC, S, most)...]
where the time goes in v4:
time: 167 us; the launch traced here: 166 us
  Pallas kernels  166 us (99%)
    pallas_call x1, Pallas kernels, fused(): pl.pallas_call(functools.partial(fused_kernel, (R, C, NB, N, PC, S, most)...  163 us

profile of v4, /device:TPU:0, one launch (start us, length us, event | category | flops | bytes accessed | tf_op | source)
XLA Modules:
  0.0 165.7 jit_solution(17280157642309476104)
XLA Ops:
  0.0 162.6 %shard_map.64.source = bf16[1024,1024]{1,0:T(8,128)(2,1)} custom-call(f32[4,512,1024]{2,1,0:T(8,128)} %rhs_in.1, bf16[4096,1024]{1,0:T(8,128)(2,1)} %bound_in.1, bf16[4096,4,512]{2,1,0:T(4,128)(2,1)} %border_in.1, bf16[6,1024,512]{2,1,0:T(8,128)(2,1)} %lower_in.1, bf16[4,512,1024]{2,1,0:T(8,128)(2,1)} %inv_in.1, s32[1,512]{1,0:T(1,128)} %bitcast.1), custom_call_target="tpu_custom_call" | custom-call | tf_op jit(solution)/shard_map/pallas_call | solution.py:811
  162.6 3.1 %shard_map.65 = f32[1024,1024]{1,0:T(8,128)} custom-call(bf16[1024,1024]{1,0:T(8,128)(2,1)} %shard_map.64.source), custom_call_target="tpu_custom_call" | custom-call | tf_op jit(solution)/shard_map/pallas_call | solution.py:873

commit v5 on v4

--- a/solution.py
+++ b/solution.py
@@ -726,7 +726,7 @@
     mid_lags = [min(lag, LAG_BASE) * (PC - 1) // LAG_BASE for lag in MID_LAGS]
     end_lags = [min(lag, LAG_BASE) * (PC - 1) // LAG_BASE for lag in END_LAGS]
     stages = list(zip((first, second, third, fourth, fifth, sixth), mid_lags, end_lags))
-    stages.append((seventh, PC - 1, PC - 1))
+    stages.append((seventh, end_lags[4] + 1, end_lags[4] + 1))
     stages.append((sends, S - 1, S - 1))
 
     def fill_in(t):

time: 167 us -> 171 us (1.024)
  Pallas kernels: 166 us -> 169 us
    pallas_call x1, Pallas kernels: 163 us -> 166 us  [fused(): pl.pallas_call(functools.partial(fused_kernel, (R, C, NB, N, PC, S, most)...]
where the time goes in v5:
time: 171 us; the launch traced here: 170 us
  Pallas kernels  169 us (99%)
    pallas_call x1, Pallas kernels, fused(): pl.pallas_call(functools.partial(fused_kernel, (R, C, NB, N, PC, S, most)...  166 us

profile of v5, /device:TPU:0, one launch (start us, length us, event | category | flops | bytes accessed | tf_op | source)
XLA Modules:
  0.0 169.5 jit_solution(16077479836925476233)
XLA Ops:
  0.0 166.4 %shard_map.64.source = bf16[1024,1024]{1,0:T(8,128)(2,1)} custom-call(f32[4,512,1024]{2,1,0:T(8,128)} %rhs_in.1, bf16[4096,1024]{1,0:T(8,128)(2,1)} %bound_in.1, bf16[4096,4,512]{2,1,0:T(4,128)(2,1)} %border_in.1, bf16[6,1024,512]{2,1,0:T(8,128)(2,1)} %lower_in.1, bf16[4,512,1024]{2,1,0:T(8,128)(2,1)} %inv_in.1, s32[1,512]{1,0:T(1,128)} %bitcast.1), custom_call_target="tpu_custom_call" | custom-call | tf_op jit(solution)/shard_map/pallas_call | solution.py:811
  166.4 3.1 %shard_map.65 = f32[1024,1024]{1,0:T(8,128)} custom-call(bf16[1024,1024]{1,0:T(8,128)(2,1)} %shard_map.64.source), custom_call_target="tpu_custom_call" | custom-call | tf_op jit(solution)/shard_map/pallas_call | solution.py:873
